TPU v7x, 32 devices: a whole 2x2x4 slice. The times are simulated.
32 devices in a mesh: dp: 8 (over y, x, core), mp: 4 (over z).
Axes of the slice: x: 2, y: 2, z: 4, core: 2. Of those that a mesh axis runs over, the one named last changes fastest.
Arguments:
- target_states: bfloat16 [1024, 4096], P('dp', 'mp')
- target_gain: float32 [4096], replicated, may hold values from 0.1 to 1.9
- target_head: bfloat16 [4096, 128256], P(None, ('dp', 'mp'))
- reference_states: bfloat16 [1024, 2048], P(('dp', 'mp'))
- reference_gain: float32 [2048], replicated, may hold values from 0.1 to 1.9
- reference_head: bfloat16 [2048, 128256], P(None, ('dp', 'mp'))
- token_ids: int32 [1024], P('dp'), may hold values from 0 to 128255
- reference_order: int32 [8], replicated, may hold values from 0 to 7, each once
Outputs:
- target_loss: float32 [1024], P('dp')
- reference_loss: float32 [1024], P('dp')
- reducible: float32 [8], P('dp')
Inputs may be any that keep to these rules, and one draw needn't show every extreme that they name: reference_states rows s * 128 to s * 128 + 127 belong to candidate sequence reference_order[s].
All inputs are finite; a program needn't handle non-finite values.
Results may differ from a plain program's by a relative error of at most 0.0041.
Values may be sent and summed in bfloat16 or wider, within the bound.
A program may use at most 128 MiB of HBM per device.

v0:
```python
import math
import jax
import jax.numpy as jnp
from jax import lax
from jax.sharding import PartitionSpec as P

LENGTH = 128
EPSILON = 1e-05


def normalize(states, gain):
    values = states.astype(jnp.float32)
    factor = lax.rsqrt(jnp.mean(values * values, axis=1, keepdims=True) + EPSILON)
    return (values * factor * gain[None, :]).astype(jnp.bfloat16)


def block_stats(logits, rows_id, columns):
    peak_val = jnp.max(logits, axis=1)
    exp_total = jnp.sum(jnp.exp(logits - peak_val[:, None]), axis=1)
    chosen = jnp.sum(jnp.where(columns[None, :] == rows_id[:, None], logits, 0.0), axis=1)
    return (peak_val, exp_total, chosen)


def shards(
    target_states,
    target_gain,
    target_head,
    reference_states,
    reference_gain,
    reference_head,
    token_ids,
    reference_order,
):
    vocab_width = target_head.shape[1]
    columns = lax.axis_index(("dp", "mp")) * vocab_width + jnp.arange(vocab_width, dtype=jnp.int32)
    rows_dp = target_states.shape[0]
    data_ways = lax.axis_size("dp")
    tokens = rows_dp * data_ways
    empty_float = jnp.zeros((tokens,), jnp.float32)
    empty_ids = jnp.zeros((tokens,), jnp.int32)
    gathered = lax.all_gather(target_states, "mp", axis=1, tiled=True)
    normed = normalize(gathered, target_gain)
    carry = (empty_float, empty_float, empty_float, empty_ids)
    start = jnp.int32(0)
    rows_x = lax.all_gather(normed, "dp", axis=0, tiled=True)
    rows_id = lax.all_gather(token_ids, "dp", axis=0, tiled=True)
    logits = jnp.dot(rows_x, target_head, preferred_element_type=jnp.float32)
    found = block_stats(logits, rows_id, columns) + (rows_id,)
    t_peak, t_total, t_pick, ids_all = tuple(
        (
            lax.dynamic_update_slice_in_dim(earlier, fresh_val, start, 0)
            for earlier, fresh_val in zip(carry, found)
        )
    )
    ref_normed = normalize(reference_states, reference_gain)
    ref_rows = lax.all_gather(ref_normed, ("dp", "mp"), axis=0, tiled=True)
    seq_count = tokens // LENGTH
    ref_ids = jnp.take(ids_all.reshape(seq_count, LENGTH), reference_order, axis=0).reshape(tokens)
    blocking = math.gcd(tokens, 512)

    def ref_block(packed):
        rows_x, rows_id = packed
        logits = jnp.dot(rows_x, reference_head, preferred_element_type=jnp.float32)
        return block_stats(logits, rows_id, columns)

    r_peak, r_total, r_pick = lax.map(
        ref_block,
        (ref_rows.reshape(-1, blocking, ref_rows.shape[1]), ref_ids.reshape(-1, blocking)),
    )
    r_peak = r_peak.reshape(tokens)
    r_total = r_total.reshape(tokens)
    r_pick = r_pick.reshape(tokens)
    t_max, r_max = lax.pmax((t_peak, r_peak), ("dp", "mp"))
    t_sum, t_hit, r_sum, r_hit = lax.psum(
        (t_total * jnp.exp(t_peak - t_max), t_pick, r_total * jnp.exp(r_peak - r_max), r_pick),
        ("dp", "mp"),
    )
    loss_target = t_max + jnp.log(t_sum) - t_hit
    loss_rows = r_max + jnp.log(r_sum) - r_hit
    matches = (reference_order[:, None] == jnp.arange(seq_count, dtype=jnp.int32)[None, :]).astype(
        jnp.float32
    )
    loss_reference = jnp.sum(
        matches[:, :, None] * loss_rows.reshape(seq_count, LENGTH)[:, None, :], axis=0
    ).reshape(tokens)
    first_row = lax.axis_index("dp") * rows_dp
    mine_target = lax.dynamic_slice_in_dim(loss_target, first_row, rows_dp, 0)
    mine_reference = lax.dynamic_slice_in_dim(loss_reference, first_row, rows_dp, 0)
    reducible = jnp.mean((mine_target - mine_reference).reshape(rows_dp // LENGTH, LENGTH), axis=1)
    return (mine_target, mine_reference, reducible)


def solution(mesh):
    placed = (
        P("dp", "mp"),
        P(),
        P(None, ("dp", "mp")),
        P(("dp", "mp"), None),
        P(),
        P(None, ("dp", "mp")),
        P("dp"),
        P(),
    )
    return jax.shard_map(
        shards, mesh=mesh, in_specs=placed, out_specs=(P("dp"), P("dp"), P("dp")), check_vma=False
    )
```

profile of v0, /device:TPU:0, one launch (start us, length us, event | category | flops | bytes accessed | tf_op | source)
XLA Modules:
  0.0 299.8 jit_solution(6555905454492770305)
XLA Ops:
  7.2 0.0 all-gather.5.cloned.1.call-start
  7.2 0.7 all-gather.5.cloned.1.call-update
  7.9 0.0 all-gather.9.cloned.1.call-start
  7.9 1.0 fusion.9
  9.0 1.7 fusion.11
  10.7 0.0 all-gather.9.cloned.1.call-update
  10.7 0.0 all-gather.7.cloned.1.call-start
  10.7 29.6 %all-gather.5.cloned.1.call-done = bf16[128,4096]{1,0:T(8,128)(2,1)} async-done(((bf16[128,1024]{1,0:T(8,128)(2,1)}), bf16[128,4096]{1,0:T(8,128)(2,1)}) %all-gather.5.cloned.1.call-update) | async-done | bytes 1048592 | tf_op jit(solution)/shard_map/all_gather | solution.py:41
  40.3 1.5 fusion.6
  41.8 2.6 fusion.8
  44.4 0.0 all-gather.7.cloned.1.call-update
  44.5 8.8 %all-gather = s32[8,1,128]{2,1,0:T(1,128)S(1)} all-gather(s32[1,1,128]{2,1,0:T(1,128)} %bitcast.56), channel_id=1, replica_groups=mesh['dp'=8,'mp'=4] {'dp'}, dimensions={0}, use_global_device_ids=true | all-gather | bytes 4608 | tf_op jit(solution)/shard_map/all_gather | solution.py:46
  53.3 0.7 compare_select_fusion
  54.0 0.6 gather_fusion
  54.5 0.7 compare_and_fusion
  55.2 0.1 broadcast_in_dim.48
  55.3 0.1 broadcast_bitcast_fusion
  55.4 1.3 fusion.12
  56.7 47.6 %all-gather.9.cloned.1.call-done = bf16[1024,2048]{1,0:T(8,128)(2,1)} async-done(((bf16[32,2048]{1,0:T(8,128)(2,1)}), bf16[1024,2048]{1,0:T(8,128)(2,1)}) %all-gather.9.cloned.1.call-update) | async-done | bytes 4194320 | tf_op jit(solution)/shard_map/all_gather | solution.py:56
  104.3 41.7 %while.15 = (s32[]{:T(128)}, f32[2,512]{1,0:T(2,128)S(1)}, f32[2,512]{1,0:T(2,128)S(1)}, f32[2,512]{1,0:T(2,128)S(1)}, bf16[2,512,2048]{2,1,0:T(8,128)(2,1)}, /*...) while((s32[]{:T(128)}, f32[2,512]{1,0:T(2,128)S(1)}, ...), condition=%wide.region_12.13_spmd.clone, body=%wide.region_8.12_spmd.clone.sunk | while | flops 8417700352 | bytes 34989508 | solution.py:66
  104.3 14.8 %fusion.21 = (f32[512]{0:T(512)S(1)}, f32[512,4008]{0,1:T(8,128)}) fusion(bf16[2048,4008]{0,1:T(8,128)(2,1)} %get-tuple-element.186, bf16[2,512,2048]{2,1,0:T(8,128)(2,1)} %get-tuple-element.185, s32[]{:T(128)S(6)} %copy.24), kind=kOutput, calls=%fused_computation.38.clone.1 | convolution fusion | flops 8407436800 | bytes 26724356 | tf_op jit(solution)/shard_map/while/body/eval_jaxpr/dot_general | solution.py:63
  119.2 5.1 %select_reduce_fusion.3 = (f32[512]{0:T(512)S(1)}, f32[512]{0:T(512)S(1)}) fusion(f32[512,4008]{0,1:T(8,128)} %get-tuple-element.158, s32[512]{0:T(512)S(1)} %bitcast.47, s32[4008]{0:T(1024)S(1)} %iota_add_fusion.3, f32[512]{0:T(512)S(1)} %get-tuple-element.157), kind=kLoop, calls=%fused_computation.2.clone.1 | loop fusion | flops 10259456 | bytes 8232608 | tf_op jit(solution)/shard_map/while/body/eval_jaxpr/reduce_sum | solution.py:20
  124.4 16.3 %fusion.21 = (f32[512]{0:T(512)S(1)}, f32[512,4008]{0,1:T(8,128)}) fusion(bf16[2048,4008]{0,1:T(8,128)(2,1)} %get-tuple-element.186, bf16[2,512,2048]{2,1,0:T(8,128)(2,1)} %get-tuple-element.185, s32[]{:T(128)S(6)} %copy.24), kind=kOutput, calls=%fused_computation.38.clone.1 | convolution fusion | flops 8407436800 | bytes 26724356 | tf_op jit(solution)/shard_map/while/body/eval_jaxpr/dot_general | solution.py:63
  140.7 5.3 %select_reduce_fusion.3 = (f32[512]{0:T(512)S(1)}, f32[512]{0:T(512)S(1)}) fusion(f32[512,4008]{0,1:T(8,128)} %get-tuple-element.158, s32[512]{0:T(512)S(1)} %bitcast.47, s32[4008]{0:T(1024)S(1)} %iota_add_fusion.3, f32[512]{0:T(512)S(1)} %get-tuple-element.157), kind=kLoop, calls=%fused_computation.2.clone.1 | loop fusion | flops 10259456 | bytes 8232608 | tf_op jit(solution)/shard_map/while/body/eval_jaxpr/reduce_sum | solution.py:20
  146.1 13.2 %all-gather.7.cloned.1.call-done = bf16[1024,4096]{1,0:T(8,128)(2,1)} async-done(((bf16[128,4096]{1,0:T(8,128)(2,1)}), bf16[1024,4096]{1,0:T(8,128)(2,1)}) %all-gather.7.cloned.1.call-update) | async-done | bytes 8388624 | tf_op jit(solution)/shard_map/all_gather | solution.py:45
  159.3 42.1 %fusion.14 = (f32[1024]{0:T(1024)S(1)}, f32[1024,4008]{0,1:T(8,128)}) fusion(bf16[1024,4096]{1,0:T(8,128)(2,1)} %all-gather.7.cloned.1.call-done, bf16[4096,4008]{0,1:T(8,128)(2,1)} %param.12), kind=kOutput, calls=%fused_computation.39 | convolution fusion | flops 33625645056 | bytes 57643008 | tf_op jit(solution)/shard_map/dot_general | solution.py:47
  201.4 39.5 %all-reduce.1 = (f32[1024]{0:T(1024)S(1)}, f32[1024]{0:T(1024)S(1)}) all-reduce(f32[1024]{0:T(1024)S(1)} %get-tuple-element.100, f32[1024]{0:T(1024)S(1)} %bitcast.48), channel_id=1, replica_groups=mesh['dp'=8,'mp'=4] {'dp','mp'}, use_global_device_ids=true, to_apply=%region_2.0 | all-reduce | flops 2048 | bytes 16384 | tf_op jit(solution)/shard_map/pmax | solution.py:73
  240.9 0.0 copy-start
  240.9 8.0 %exponential_reduce_fusion.1 = (f32[1024]{0:T(1024)S(1)}, f32[1024]{0:T(1024)S(1)}) fusion(f32[1024,4008]{0,1:T(8,128)} %get-tuple-element.101, f32[1024]{0:T(1024)S(1)} %get-tuple-element.100, s32[1024]{0:T(1024)S(1)} %bitcast.43, s32[4008]{0:T(1024)S(1)} %iota_add_fusion.1), kind=kLoop, calls=%fused_computation.11 | loop fusion | flops 20518912 | bytes 16449184 | tf_op jit(solution)/shard_map/reduce_sum | solution.py:19
  248.9 41.2 %all-reduce = (f32[1024]{0:T(1024)S(1)}, f32[1024]{0:T(1024)S(1)}, f32[1024]{0:T(1024)S(1)}, f32[1024]{0:T(1024)S(1)}) all-reduce(f32[1024]{0:T(1024)S(1)} %get-tuple-element.72, f32[1024]{0:T(1024)S(1)} %get-tuple-element.103, f32[1024]{0:T(1024)S(1)} %bitcast.50, ...), channel_id=1, replica_groups=mesh['dp'=8,'mp'=4] {'dp','mp'}, use_global_device_ids=true, to_apply=%region_6.7 | all-reduce | flops 4096 | bytes 32768 | tf_op jit(solution)/shard_map/psum | solution.py:74
  290.2 0.0 copy-done
  290.2 0.1 multiply_reduce_fusion
  290.3 1.2 subtract_reduce_fusion
  (25 shorter events, 0.3 us)
Async XLA Ops:
  7.2 33.1 %all-gather.5.cloned.1.call-start = ((), (), s32[]{:S(2)}) async-start(), calls=%async_computation | async-start | bytes 1310720 | tf_op jit(solution)/shard_map/all_gather | solution.py:41
  7.9 96.4 %all-gather.9.cloned.1.call-start = ((), (), s32[]{:S(2)}) async-start(), calls=%async_computation.2 | async-start | bytes 4325376 | tf_op jit(solution)/shard_map/all_gather | solution.py:56
  10.7 148.6 %all-gather.7.cloned.1.call-start = ((), (), s32[]{:S(2)}) async-start(), calls=%async_computation.1 | async-start | bytes 9437184 | tf_op jit(solution)/shard_map/all_gather | solution.py:45
  240.9 49.3 %copy-start = (f32[8,8]{1,0:T(8,128)S(1)}, f32[8,8]{1,0:T(8,128)}, u32[]{:S(2)}) copy-start(f32[8,8]{1,0:T(8,128)} %fusion.12) | copy-start | bytes 772
Sparse Core Ops, SparseCore 0:
  9.5 30.6 all-gather.4
  43.3 60.9 all-gather.8
  106.2 53.0 all-gather.6
where the time goes:
time: 300 us
  waiting for transfers between devices  91.1 us (30%)
  blocking collectives  89.6 us (30%)
  matrix products  73.2 us (24%)
  other arithmetic  29.1 us (10%)
  between operations  15.6 us (5%)
    all_gather x1, waiting for transfers between devices, shards(): ref_rows = lax.all_gather(ref_normed, ('dp', 'mp'), axis=0, tiled=True)  47.6 us
    dot_general x1, matrix products, shards(): logits = jnp.dot(rows_x, target_head, preferred_element_type=jnp.float32)  42.1 us
    psum x1, blocking collectives, shards(): lax.psum((t_total * jnp.exp(t_peak - t_max), t_pick, r_total * jnp.exp(r_...  41.2 us
    pmax x1, blocking collectives, shards(): t_max, r_max = lax.pmax((t_peak, r_peak), ('dp', 'mp'))  39.5 us
    dot_general x2, matrix products, ref_block(): logits = jnp.dot(rows_x, reference_head, preferred_element_type=jnp.float32)  31.1 us
    all_gather x1, waiting for transfers between devices, shards(): gathered = lax.all_gather(target_states, 'mp', axis=1, tiled=True)  29.6 us
    all_gather x1, waiting for transfers between devices, shards(): rows_x = lax.all_gather(normed, 'dp', axis=0, tiled=True)  13.2 us
    reduce_sum x2, other arithmetic, block_stats(): jnp.sum(jnp.where(columns[None, :] == rows_id[:, None], logits, 0.0), axi...  10.3 us
  transfers between devices with their start and end apart: 3, of which 3 were waited for; matrix products, arithmetic and copies ran while one was open for 17% of the time, Pallas kernels for 0%

commit v1 on v0

--- a/solution.py
+++ b/solution.py
@@ -6,6 +6,17 @@
 
 LENGTH = 128
 EPSILON = 1e-05
+
+
+def around_the_ring(x, axis, dim):
+    n_dev = lax.axis_size(axis)
+    right = [(i, (i + 1) % n_dev) for i in range(n_dev)]
+    parts = [x]
+    for stride in range(1, n_dev):
+        parts = [lax.ppermute(parts[0], axis, right), *parts]
+    full = jnp.concatenate(parts, axis=dim)
+    shift = (lax.axis_index(axis) + 1) * parts[-1].shape[dim]
+    return jnp.roll(full, shift, axis=dim)
 
 
 def normalize(states, gain):
@@ -38,7 +49,7 @@
     tokens = rows_dp * data_ways
     empty_float = jnp.zeros((tokens,), jnp.float32)
     empty_ids = jnp.zeros((tokens,), jnp.int32)
-    gathered = lax.all_gather(target_states, "mp", axis=1, tiled=True)
+    gathered = around_the_ring(target_states, "mp", 1)
     normed = normalize(gathered, target_gain)
     carry = (empty_float, empty_float, empty_float, empty_ids)
     start = jnp.int32(0)

time: 300 us -> 275 us (0.917)
  waiting for transfers between devices: 91.1 us -> 65.7 us
  other arithmetic: 29.1 us -> 24.8 us
  starting transfers between devices: 0.12 us -> 3.19 us
    all_gather x1 -> x0, waiting for transfers between devices: 29.6 us -> none  [shards(): gathered = lax.all_gather(target_states, 'mp', axis=1, tiled=True)]
    ppermute x0 -> x3, waiting for transfers between devices: none -> 28.1 us  [around_the_ring(): parts = [lax.ppermute(parts[0], axis, right), *parts]]
    all_gather x1, waiting for transfers between devices: 47.6 us -> 24.4 us  [shards(): ref_rows = lax.all_gather(ref_normed, ('dp', 'mp'), axis=0, tiled=True)]
    ppermute x0 -> x3, starting transfers between devices: none -> 3.11 us  [around_the_ring(): parts = [lax.ppermute(parts[0], axis, right), *parts]]
  transfers between devices with their start and end apart: 3 -> 5, of which waited for: 3 -> 5; matrix products, arithmetic and copies ran while one was open for 17% -> 17% of each run, Pallas kernels for 0% -> 0%
where the time goes in v1:
time: 275 us; the launch traced here: 274 us
  blocking collectives  89.2 us (32%)
  matrix products  73.2 us (27%)
  waiting for transfers between devices  65.7 us (24%)
  other arithmetic  24.8 us (9%)
  between operations  16 us (6%)
  starting transfers between devices  3.19 us (1%)
    dot_general x1, matrix products, shards(): logits = jnp.dot(rows_x, target_head, preferred_element_type=jnp.float32)  42.1 us
    psum x1, blocking collectives, shards(): lax.psum((t_total * jnp.exp(t_peak - t_max), t_pick, r_total * jnp.exp(r_...  41.3 us
    pmax x1, blocking collectives, shards(): t_max, r_max = lax.pmax((t_peak, r_peak), ('dp', 'mp'))  39.5 us
    dot_general x2, matrix products, ref_block(): logits = jnp.dot(rows_x, reference_head, preferred_element_type=jnp.float32)  31.1 us
    ppermute x3, waiting for transfers between devices, around_the_ring(): parts = [lax.ppermute(parts[0], axis, right), *parts]  28.1 us
    all_gather x1, waiting for transfers between devices, shards(): ref_rows = lax.all_gather(ref_normed, ('dp', 'mp'), axis=0, tiled=True)  24.4 us
    all_gather x1, waiting for transfers between devices, shards(): rows_x = lax.all_gather(normed, 'dp', axis=0, tiled=True)  13.2 us
    reduce_sum x2, other arithmetic, block_stats(): jnp.sum(jnp.where(columns[None, :] == rows_id[:, None], logits, 0.0), axi...  10.3 us
  transfers between devices with their start and end apart: 5, of which 5 were waited for; matrix products, arithmetic and copies ran while one was open for 17% of the time, Pallas kernels for 0%

profile of v1, /device:TPU:0, one launch (start us, length us, event | category | flops | bytes accessed | tf_op | source)
XLA Modules:
  0.0 274.4 jit_solution(16019566338811771452)
XLA Ops:
  7.2 0.0 copy-start
  7.2 0.0 copy-start.1
  7.2 0.0 all-gather.6.cloned.1.call-start
  7.2 1.1 fusion.9
  8.3 1.7 fusion.11
  10.0 0.0 all-gather.6.cloned.1.call-update
  10.0 0.0 all-gather.4.cloned.1.call-start
  10.0 3.1 %collective-permute-start = (bf16[128,1024]{1,0:T(8,128)(2,1)}, bf16[128,1024]{1,0:T(8,128)(2,1)S(1)}, u32[]{:S(2)}, u32[]{:S(2)}) collective-permute-start(bf16[128,1024]{1,0:T(8,128)(2,1)} %param.10), channel_id=1, source_target_pairs={{0,1},{1,2},{2,3},{3,0},{4,5},{5,6},{6,7},{7,4},{8,9},{9,10},{10,1... | collective-permute-start | bytes 786440 | tf_op jit(solution)/shard_map/ppermute | solution.py:16
  13.2 8.5 %collective-permute-done = bf16[128,1024]{1,0:T(8,128)(2,1)S(1)} collective-permute-done((bf16[128,1024]{1,0:T(8,128)(2,1)}, bf16[128,1024]{1,0:T(8,128)(2,1)S(1)}, u32[]{:S(2)}, u32[]{:S(2)}) %collective-permute-start) | collective-permute-done | bytes 262176 | tf_op jit(solution)/shard_map/ppermute | solution.py:16
  21.7 0.0 collective-permute-start.1
  21.7 11.4 %collective-permute-done.1 = bf16[128,1024]{1,0:T(8,128)(2,1)S(1)} collective-permute-done((bf16[128,1024]{1,0:T(8,128)(2,1)S(1)}, bf16[128,1024]{1,0:T(8,128)(2,1)S(1)}, u32[]{:S(2)}, u32[]{:S(2)}) %collective-permute-start.1) | collective-permute-done | bytes 262176 | tf_op jit(solution)/shard_map/ppermute | solution.py:16
  33.1 0.0 collective-permute-start.2
  33.1 0.0 copy-start.3
  33.1 0.0 copy-start.4
  33.1 8.2 %collective-permute-done.2 = bf16[128,1024]{1,0:T(8,128)(2,1)S(1)} collective-permute-done((bf16[128,1024]{1,0:T(8,128)(2,1)S(1)}, bf16[128,1024]{1,0:T(8,128)(2,1)S(1)}, u32[]{:S(2)}, u32[]{:S(2)}) %collective-permute-start.2) | collective-permute-done | bytes 262176 | tf_op jit(solution)/shard_map/ppermute | solution.py:16
  41.4 1.0 constant_dynamic-update-slice_fusion.4
  42.5 0.0 copy-done
  42.5 0.3 fusion.6
  42.8 0.0 copy-done.1
  42.8 1.4 fusion.8
  44.2 0.0 all-gather.4.cloned.1.call-update
  44.2 0.0 copy-done.3
  44.3 8.4 %all-gather = s32[8,1,128]{2,1,0:T(1,128)S(1)} all-gather(s32[1,1,128]{2,1,0:T(1,128)S(1)} %bitcast.56), channel_id=1, replica_groups=mesh['dp'=8,'mp'=4] {'dp'}, dimensions={0}, use_global_device_ids=true | all-gather | bytes 4608 | tf_op jit(solution)/shard_map/all_gather | solution.py:57
  52.7 0.0 copy-done.4
  52.7 0.6 gather_fusion
  53.3 0.1 broadcast_in_dim.48
  53.4 0.1 broadcast_bitcast_fusion
  53.4 0.7 fusion.12
  54.1 24.4 %all-gather.6.cloned.1.call-done = bf16[1024,2048]{1,0:T(8,128)(2,1)} async-done(((bf16[32,2048]{1,0:T(8,128)(2,1)}), bf16[1024,2048]{1,0:T(8,128)(2,1)}) %all-gather.6.cloned.1.call-update) | async-done | bytes 4194320 | tf_op jit(solution)/shard_map/all_gather | solution.py:67
  78.5 41.7 %while.15 = (s32[]{:T(128)}, f32[2,512]{1,0:T(2,128)S(1)}, f32[2,512]{1,0:T(2,128)S(1)}, f32[2,512]{1,0:T(2,128)S(1)}, bf16[2,512,2048]{2,1,0:T(8,128)(2,1)}, /*...) while((s32[]{:T(128)}, f32[2,512]{1,0:T(2,128)S(1)}, ...), condition=%wide.region_12.13_spmd.clone, body=%wide.region_8.12_spmd.clone.sunk | while | flops 8417700352 | bytes 34989508 | solution.py:77
  78.5 14.8 %fusion.21 = (f32[512]{0:T(512)S(1)}, f32[512,4008]{0,1:T(8,128)}) fusion(bf16[2048,4008]{0,1:T(8,128)(2,1)} %get-tuple-element.186, bf16[2,512,2048]{2,1,0:T(8,128)(2,1)} %get-tuple-element.185, s32[]{:T(128)S(6)} %copy.31), kind=kOutput, calls=%fused_computation.46.clone.1 | convolution fusion | flops 8407436800 | bytes 26724356 | tf_op jit(solution)/shard_map/while/body/eval_jaxpr/dot_general | solution.py:74
  93.4 5.1 %select_reduce_fusion.3 = (f32[512]{0:T(512)S(1)}, f32[512]{0:T(512)S(1)}) fusion(f32[512,4008]{0,1:T(8,128)} %get-tuple-element.158, s32[512]{0:T(512)S(1)} %bitcast.47, s32[4008]{0:T(1024)S(1)} %iota_add_fusion.3, f32[512]{0:T(512)S(1)} %get-tuple-element.157), kind=kLoop, calls=%fused_computation.2.clone.1 | loop fusion | flops 10259456 | bytes 8232608 | tf_op jit(solution)/shard_map/while/body/eval_jaxpr/reduce_sum | solution.py:31
  98.6 16.3 %fusion.21 = (f32[512]{0:T(512)S(1)}, f32[512,4008]{0,1:T(8,128)}) fusion(bf16[2048,4008]{0,1:T(8,128)(2,1)} %get-tuple-element.186, bf16[2,512,2048]{2,1,0:T(8,128)(2,1)} %get-tuple-element.185, s32[]{:T(128)S(6)} %copy.31), kind=kOutput, calls=%fused_computation.46.clone.1 | convolution fusion | flops 8407436800 | bytes 26724356 | tf_op jit(solution)/shard_map/while/body/eval_jaxpr/dot_general | solution.py:74
  114.9 5.3 %select_reduce_fusion.3 = (f32[512]{0:T(512)S(1)}, f32[512]{0:T(512)S(1)}) fusion(f32[512,4008]{0,1:T(8,128)} %get-tuple-element.158, s32[512]{0:T(512)S(1)} %bitcast.47, s32[4008]{0:T(1024)S(1)} %iota_add_fusion.3, f32[512]{0:T(512)S(1)} %get-tuple-element.157), kind=kLoop, calls=%fused_computation.2.clone.1 | loop fusion | flops 10259456 | bytes 8232608 | tf_op jit(solution)/shard_map/while/body/eval_jaxpr/reduce_sum | solution.py:31
  120.3 13.2 %all-gather.4.cloned.1.call-done = bf16[1024,4096]{1,0:T(8,128)(2,1)} async-done(((bf16[128,4096]{1,0:T(8,128)(2,1)}), bf16[1024,4096]{1,0:T(8,128)(2,1)}) %all-gather.4.cloned.1.call-update) | async-done | bytes 8388624 | tf_op jit(solution)/shard_map/all_gather | solution.py:56
  133.5 42.1 %fusion.14 = (f32[1024]{0:T(1024)S(1)}, f32[1024,4008]{0,1:T(8,128)}) fusion(bf16[1024,4096]{1,0:T(8,128)(2,1)} %all-gather.4.cloned.1.call-done, bf16[4096,4008]{0,1:T(8,128)(2,1)} %param.12), kind=kOutput, calls=%fused_computation.47 | convolution fusion | flops 33625645056 | bytes 57643008 | tf_op jit(solution)/shard_map/dot_general | solution.py:58
  175.6 39.5 %all-reduce.1 = (f32[1024]{0:T(1024)S(1)}, f32[1024]{0:T(1024)S(1)}) all-reduce(f32[1024]{0:T(1024)S(1)} %get-tuple-element.100, f32[1024]{0:T(1024)S(1)} %bitcast.48), channel_id=1, replica_groups=mesh['dp'=8,'mp'=4] {'dp','mp'}, use_global_device_ids=true, to_apply=%region_2.3 | all-reduce | flops 2048 | bytes 16384 | tf_op jit(solution)/shard_map/pmax | solution.py:84
  215.1 0.0 copy-start.2
  215.1 8.0 %exponential_reduce_fusion.1 = (f32[1024]{0:T(1024)S(1)}, f32[1024]{0:T(1024)S(1)}) fusion(f32[1024,4008]{0,1:T(8,128)} %get-tuple-element.101, f32[1024]{0:T(1024)S(1)} %get-tuple-element.100, s32[1024]{0:T(1024)S(1)} %bitcast.43, s32[4008]{0:T(1024)S(1)} %iota_add_fusion.1), kind=kLoop, calls=%fused_computation.11 | loop fusion | flops 20518912 | bytes 16449184 | tf_op jit(solution)/shard_map/reduce_sum | solution.py:30
  223.2 41.3 %all-reduce = (f32[1024]{0:T(1024)S(1)}, f32[1024]{0:T(1024)S(1)}, f32[1024]{0:T(1024)S(1)}, f32[1024]{0:T(1024)S(1)}) all-reduce(f32[1024]{0:T(1024)S(1)} %get-tuple-element.72, f32[1024]{0:T(1024)S(1)} %get-tuple-element.103, f32[1024]{0:T(1024)S(1)} %bitcast.50, ...), channel_id=1, replica_groups=mesh['dp'=8,'mp'=4] {'dp','mp'}, use_global_device_ids=true, to_apply=%region_6.7 | all-reduce | flops 4096 | bytes 32768 | tf_op jit(solution)/shard_map/psum | solution.py:85
  264.4 0.0 copy-done.2
  264.5 0.1 multiply_reduce_fusion
  264.5 1.2 subtract_reduce_fusion
  (34 shorter events, 0.5 us)
Async XLA Ops:
  7.2 35.3 %copy-start = (bf16[128,1024]{1,0:T(8,128)(2,1)S(1)}, bf16[128,1024]{1,0:T(8,128)(2,1)}, u32[]{:S(2)}) copy-start(bf16[128,1024]{1,0:T(8,128)(2,1)} %param.10) | copy-start | bytes 786436
  7.2 35.6 %copy-start.1 = (f32[4096]{0:T(1024)S(1)}, f32[4096]{0:T(1024)}, u32[]{:S(2)}) copy-start(f32[4096]{0:T(1024)} %param.11) | copy-start | bytes 49156
  7.2 71.3 %all-gather.6.cloned.1.call-start = ((), (), s32[]{:S(2)}) async-start(), calls=%async_computation.1 | async-start | bytes 4325376 | tf_op jit(solution)/shard_map/all_gather | solution.py:67
  10.0 123.5 %all-gather.4.cloned.1.call-start = ((), (), s32[]{:S(2)}) async-start(), calls=%async_computation | async-start | bytes 9437184 | tf_op jit(solution)/shard_map/all_gather | solution.py:56
  10.0 11.6 %collective-permute-start = (bf16[128,1024]{1,0:T(8,128)(2,1)}, bf16[128,1024]{1,0:T(8,128)(2,1)S(1)}, u32[]{:S(2)}, u32[]{:S(2)}) collective-permute-start(bf16[128,1024]{1,0:T(8,128)(2,1)} %param.10), channel_id=1, source_target_pairs={{0,1},{1,2},{2,3},{3,0},{4,5},{5,6},{6,7},{7,4},{8,9},{9,10},{10,1... | collective-permute-start | bytes 786440 | tf_op jit(solution)/shard_map/ppermute | solution.py:16
  21.7 11.4 %collective-permute-start.1 = (bf16[128,1024]{1,0:T(8,128)(2,1)S(1)}, bf16[128,1024]{1,0:T(8,128)(2,1)S(1)}, u32[]{:S(2)}, u32[]{:S(2)}) collective-permute-start(bf16[128,1024]{1,0:T(8,128)(2,1)S(1)} %collective-permute-done), channel_id=1, source_target_pairs={{0,1},{1,2},{2,3},{3,0},{4,5},{5,6},{6,7},{7,4},{8,9},{9,10},{10,1... | collective-permute-start | bytes 786440 | tf_op jit(solution)/shard_map/ppermute | solution.py:16
  33.1 8.2 %collective-permute-start.2 = (bf16[128,1024]{1,0:T(8,128)(2,1)S(1)}, bf16[128,1024]{1,0:T(8,128)(2,1)S(1)}, u32[]{:S(2)}, u32[]{:S(2)}) collective-permute-start(bf16[128,1024]{1,0:T(8,128)(2,1)S(1)} %collective-permute-done.1), channel_id=1, source_target_pairs={{0,1},{1,2},{2,3},{3,0},{4,5},{5,6},{6,7},{7,4},{8,9},{9,10},{10,1... | collective-permute-start | bytes 786440 | tf_op jit(solution)/shard_map/ppermute | solution.py:16
  33.1 11.1 %copy-start.3 = (s32[128]{0:T(128)S(1)}, s32[128]{0:T(128)}, u32[]{:S(2)}) copy-start(s32[128]{0:T(128)} %param.16) | copy-start | bytes 1540
  33.1 19.6 %copy-start.4 = (s32[8]{0:T(128)S(1)}, s32[8]{0:T(128)}, u32[]{:S(2)}) copy-start(s32[8]{0:T(128)} %param.17) | copy-start | bytes 100
  215.1 49.3 %copy-start.2 = (f32[8,8]{1,0:T(8,128)S(1)}, f32[8,8]{1,0:T(8,128)}, u32[]{:S(2)}) copy-start(f32[8,8]{1,0:T(8,128)} %fusion.12) | copy-start | bytes 772
Sparse Core Ops, SparseCore 0:
  11.0 67.4 all-gather.5
  80.4 53.0 all-gather.3
